TPU v7x, 32 devices: a whole 2x2x4 slice. The times are simulated.
32 devices in a mesh: rows: 4 (over y, x), pairs: 8 (over z, core).
Axes of the slice: x: 2, y: 2, z: 4, core: 2. Of those that a mesh axis runs over, the one named last changes fastest.
Arguments:
- latent: bfloat16 [8192, 3072], P('rows', 'pairs'), as said below
Outputs:
- rotated_latent: bfloat16 [8192, 3072], P('rows', 'pairs')
Inputs may be any that keep to these rules, and one draw needn't show every extreme that they name: `latent`: finite real entries.
All inputs are finite; a program needn't handle non-finite values.
Results may differ from a plain program's by a relative error of at most 0.0065.
Values may be sent and summed in bfloat16 or wider, within the bound.
No kernel may reach another device: no remote copies, remote signals or barrier semaphores. Data moves between devices by JAX's collectives and lax.ppermute only.
A program may use at most 64 MiB of HBM per device.

v0:
```python
import functools
import math

import jax
import jax.numpy as jnp
import numpy as np
from jax import lax
from jax.experimental import pallas as pl
from jax.experimental.pallas import tpu as pltpu
from jax.sharding import PartitionSpec as P


F32, BF16 = jnp.float32, jnp.bfloat16
LANES = 128


def polar_coefficients():
    c = 1.5 / math.sqrt(65.0)
    mul, sub = np.polynomial.polynomial.polymul, np.polynomial.polynomial.polysub
    n = np.array([c * c, c * c])
    u = np.array([1.5 - 0.5 * c * c, -0.5 * c * c])
    return [float(v) for v in c * sub(1.5 * u, 0.5 * mul(n, mul(u, mul(u, u))))]


COEF = polar_coefficients()


def window(half):
    return -(-half // LANES) * LANES


def dot(a, b, contract):
    return lax.dot_general(a, b, ((contract[:1], contract[1:]), ((), ())), preferred_element_type=F32)


def low(a):
    return a.astype(BF16)


def params():
    return pltpu.CompilerParams(vmem_limit_bytes=16 << 20)


def whole(n):
    return [pl.BlockSpec(memory_space=pltpu.VMEM)] * n


def pieces(rows, n):
    return [slice(i * (rows // n), (i + 1) * (rows // n)) for i in range(n)]


def spans(*lists):
    cuts = {0}
    for blocks in lists:
        stop = 0
        for block in blocks:
            stop += block.shape[0]
            cuts.add(stop)
    cuts = sorted(cuts)
    return list(zip(cuts[:-1], cuts[1:]))


def span(blocks, start, stop):
    for block in blocks:
        if start < block.shape[0]:
            return block.at[start:stop]
        start, stop = start - block.shape[0], stop - block.shape[0]


def blocks_of(cols, sizes):
    return [jax.ShapeDtypeStruct((n, cols), BF16) for n in sizes]


def pack_window(top, bot, half):
    w = top.shape[1]
    lane = lax.broadcasted_iota(jnp.int32, top.shape, 1)
    return jnp.where(lane < half, pltpu.roll(top, half, 1), 0.0), jnp.where(lane >= w - half, bot, 0.0)


def unpack_window(packed):
    cols = packed.shape[1]
    half = cols // 2
    w = window(half)
    return jnp.concatenate([pltpu.roll(packed[:, :w], w - half, 1), packed[:, cols - w :]], axis=0)


def pack_stats(g_ref, cross, norms):
    half, _ = cross.shape
    h = half // 2
    packed_store(g_ref, slice(0, h), *pack_window(cross[:h], cross[h:], half), half)
    row = lax.broadcasted_iota(jnp.int32, (8, g_ref.shape[1]), 0)
    rest = norms - low(norms).astype(F32)
    g_ref[h:] = low(jnp.where(row == 0, norms, jnp.where(row == 1, rest, 0.0)))


def stats_shape(cols):
    return jax.ShapeDtypeStruct((cols // 4 + 8, cols), BF16)


def taken_kernel(x_hbm, raw_ref, sem):
    rows, k = x_hbm.shape[0], raw_ref.shape[0] // 2
    copies = [
        pltpu.make_async_copy(x_hbm.at[stop - k : stop, :], raw_ref.at[i * k : (i + 1) * k, :], sem.at[i])
        for i, stop in enumerate((rows // 2, rows))
    ]
    for copy in copies:
        copy.start()
    for copy in copies:
        copy.wait()


def taken(x, k):
    cols = x.shape[1]
    return pl.pallas_call(
        taken_kernel,
        in_specs=[pl.BlockSpec(memory_space=pltpu.HBM)],
        out_specs=whole(1)[0],
        out_shape=jax.ShapeDtypeStruct((2 * k, cols), BF16),
        scratch_shapes=[pltpu.SemaphoreType.DMA((2,))],
        cost_estimate=pl.CostEstimate(flops=0, bytes_accessed=8 * k * cols, transcendentals=0),
        compiler_params=params(),
        name="taken",
    )(pltpu.with_memory_space_constraint(x, pltpu.HBM))


def gram_kernel(n, x_ref, g_ref):
    rows, cols = x_ref.shape
    half = cols // 2
    w = window(half)
    cross, norms = jnp.zeros((w, w), F32), jnp.zeros((1, cols), F32)
    for r in pieces(rows, n):
        x = x_ref[r, :]
        cross += dot(x[:, :w], x[:, cols - w :], (0, 0))
        xf = x.astype(F32)
        norms += jnp.sum(xf * xf, axis=0, keepdims=True)
    pack_stats(g_ref, cross[:half], norms)


def gram(x, n):
    rows, cols = x.shape
    w = window(cols // 2)
    return pl.pallas_call(
        functools.partial(gram_kernel, n),
        in_specs=whole(1),
        out_specs=whole(1)[0],
        out_shape=stats_shape(cols),
        cost_estimate=pl.CostEstimate(flops=2 * rows * w * w, bytes_accessed=2 * rows * cols, transcendentals=0),
        compiler_params=params(),
        name="gram",
    )(x)


def gram_pair_kernel(n_a, *refs):
    a_refs, b_refs, g_ref = refs[:n_a], refs[n_a:-1], refs[-1]
    cols = g_ref.shape[1]
    half = cols // 2
    w = window(half)
    pad, o = w - half, cols - w
    top, bot = jnp.zeros((w, w), F32), jnp.zeros((w, w), F32)
    norm_a, norm_b = jnp.zeros((1, cols), F32), jnp.zeros((1, cols), F32)
    for start, stop in spans(a_refs, b_refs):
        a, b = span(a_refs, start, stop)[...], span(b_refs, start, stop)[...]
        top += dot(a[:, :w], b[:, :w], (0, 0))
        bot += dot(a[:, o:], b[:, o:], (0, 0))
        af, bf = a.astype(F32), b.astype(F32)
        norm_a += jnp.sum(af * af, axis=0, keepdims=True)
        norm_b += jnp.sum(bf * bf, axis=0, keepdims=True)
    cross = pltpu.roll(top[:half], pad, 1) + bot[pad:]
    s, t = jnp.broadcast_to(norm_a, (8, cols)), jnp.broadcast_to(norm_b, (8, cols))
    left = s + jnp.concatenate([pltpu.roll(s[:, o:], half, 1), jnp.zeros((8, o), F32)], axis=1)
    right = t + jnp.concatenate([jnp.zeros((8, o), F32), pltpu.roll(t[:, :w], pad, 1)], axis=1)
    lane = lax.broadcasted_iota(jnp.int32, (8, cols), 1)
    pack_stats(g_ref, cross, jnp.where(lane < half, left, right)[:1])


def gram_pair(a, b):
    cols = a[0].shape[1]
    rows = sum(v.shape[0] for v in a)
    w = window(cols // 2)
    return pl.pallas_call(
        functools.partial(gram_pair_kernel, len(a)),
        in_specs=whole(len(a) + len(b)),
        out_specs=whole(1)[0],
        out_shape=stats_shape(cols),
        cost_estimate=pl.CostEstimate(flops=4 * rows * w * w, bytes_accessed=4 * rows * cols, transcendentals=0),
        compiler_params=params(),
        name="gram_pair",
    )(*a, *b)


def cross_of(parts):
    total = sum((p[...].astype(F32) for p in parts[1:]), parts[0][...].astype(F32))
    cols = total.shape[1]
    half = cols // 2
    w = window(half)
    pad, h = w - half, half // 2
    cross = unpack_window(total[:h])
    norms = total[h:] + pltpu.roll(total[h:], 7, 0)
    left = jnp.transpose(norms[:, :w])[:half, :1]
    corr = cross * (lax.rsqrt(left) * lax.rsqrt(norms[:1, cols - w :]))
    lane = lax.broadcasted_iota(jnp.int32, corr.shape, 1)
    corr = jnp.where(lane >= pad, corr, 0.0)
    size = jnp.sqrt(2.0 * jnp.sum(corr * corr) + 1e-12)
    return filled(corr * (8.0 / size))


def filled(x):
    half, w = x.shape
    return jnp.concatenate([x, jnp.zeros((w - half, w), F32)], axis=0) if w > half else x


def split(a):
    high = low(a)
    return high, low(a - high.astype(F32))


def split_dot(a, b, contract=(1, 0)):
    return dot(a[0], b[0], contract) + (dot(a[0], b[1], contract) + dot(a[1], b[0], contract))


def minus_constant(k):
    words = split(k)
    k2 = split_dot(words, words)
    return COEF[1] * k + COEF[2] * k2 + dot(low(k2), low(COEF[3] * k + COEF[4] * k2), (1, 0))


def word_dot(x, delta, contract):
    high, rest = split(delta)
    return dot(x, high, contract) + dot(x, rest, contract)


def eye_at(w, first, stop):
    r = lax.broadcasted_iota(jnp.int32, (w, w), 0)
    c = lax.broadcasted_iota(jnp.int32, (w, w), 1)
    return (r == c) & (r >= first) & (r < stop)


def left_columns(x, half):
    w = x.shape[1]
    xb = low(x)
    k = dot(xb, xb, (1, 1))
    delta = minus_constant(k)
    upper = delta + jnp.where(eye_at(w, 0, half), COEF[0], 0.0)
    lower = -(COEF[0] * jnp.transpose(x) + word_dot(xb, delta, (0, 0)))
    return low(jnp.concatenate([upper[:half], lower[w - half :]], axis=0))


def right_columns(x, half):
    w = x.shape[1]
    xb = low(x)
    k = dot(xb, xb, (0, 0))
    delta = minus_constant(k)
    upper = COEF[0] * x + word_dot(xb, delta, (1, 0))
    lower = delta + jnp.where(eye_at(w, w - half, w), COEF[0], 0.0)
    return low(jnp.concatenate([upper[:half], lower[w - half :]], axis=0))


def moved(q, by):
    return low(pltpu.roll(q.astype(F32), by, 1)) if by else q


def packed_store(ref, rows, top, bot, half):
    w = top.shape[1]
    o = 2 * half - w
    ref[rows, :o] = low(top[:, :o])
    if w > o:
        ref[rows, o:w] = low(top[:, o:] + bot[:, : w - o])
    ref[rows, w:] = low(bot[:, w - o :])


def rotate_into(refs, x_ref, q_top, q_bot, base=0):
    rows, half = x_ref.shape[0] // 2, x_ref.shape[1] // 2
    for start, stop in spans(refs):
        top = dot(x_ref[base + start : base + stop, :], q_top, (1, 0))
        bot = dot(x_ref[rows + base + start : rows + base + stop, :], q_bot, (1, 0))
        packed_store(span(refs, start, stop), slice(None), top, bot, half)


def rounded_factor(s_ref, s):
    h, cols = s_ref.shape
    packed_store(s_ref, slice(None), *pack_window(s[:h], s[h : 2 * h], cols // 2), cols // 2)


def own_share(s_ref, n):
    s = s_ref[...].astype(F32)
    h = s.shape[0] // n
    me, share = lax.axis_index("rows"), s[:h]
    for k in range(1, n):
        share = jnp.where(me == k, s[k * h : (k + 1) * h], share)
    return low(share)


def joined(share_refs):
    shares = [ref[...].astype(F32) for ref in share_refs]
    if len(shares) == 1:
        return shares[0]
    me, rows = lax.axis_index("rows"), []
    for at in range(len(shares)):
        row = shares[0]
        for k in range(1, len(shares)):
            row = jnp.where(me == at ^ k, shares[k], row)
        rows.append(row)
    return jnp.concatenate(rows, axis=0)


def shared(cols):
    n = lax.axis_size("rows")
    return n if n <= 4 and not n & (n - 1) and (cols // 4) % (8 * n) == 0 else 1


def factor(*share_refs):
    s = unpack_window(joined(share_refs))
    half, w = s.shape
    lane = lax.broadcasted_iota(jnp.int32, s.shape, 1)
    return filled(jnp.where(lane >= w - half, s, 0.0)), half


def left_pair(s, half):
    left = left_columns(s, half)
    return left, moved(left, s.shape[1] - half)


def rotor_kernel(n_parts, *refs):
    parts = refs[:n_parts]
    x_ref, s_ref, share_ref, *a_refs = refs[n_parts:]
    s = cross_of(parts)
    rounded_factor(s_ref, s)
    share_ref[...] = own_share(s_ref, s_ref.shape[0] // share_ref.shape[0])
    rotate_into(a_refs, x_ref, *left_pair(low(s).astype(F32), x_ref.shape[1] // 2))


def rotor(parts, x, sizes):
    _, cols = x.shape
    w = window(cols // 2)
    s, share, *a = pl.pallas_call(
        functools.partial(rotor_kernel, len(parts)),
        in_specs=whole(len(parts) + 1),
        out_specs=whole(2 + len(sizes)),
        out_shape=blocks_of(cols, [cols // 4, cols // 4 // shared(cols)] + sizes),
        cost_estimate=pl.CostEstimate(flops=4 * sum(sizes) * cols * w, bytes_accessed=6 * sum(sizes) * cols, transcendentals=0),
        compiler_params=params(),
        name="rotor",
    )(*parts, x)
    return s, share, a


def tail_kernel(*refs):
    *s_refs, x_ref, a_ref = refs
    rotate_into([a_ref], x_ref, *left_pair(*factor(*s_refs)), base=x_ref.shape[0] // 2 - a_ref.shape[0])


def tail(s, x, k):
    cols = x.shape[1]
    w = window(cols // 2)
    return pl.pallas_call(
        tail_kernel,
        in_specs=whole(len(s) + 1),
        out_specs=whole(1)[0],
        out_shape=jax.ShapeDtypeStruct((k, cols), BF16),
        cost_estimate=pl.CostEstimate(flops=4 * k * cols * w, bytes_accessed=6 * k * cols, transcendentals=0),
        compiler_params=params(),
        name="tail",
    )(*s, x)


def rotate_kernel(s_ref, x_ref, *b_refs):
    s, half = factor(s_ref)
    right = right_columns(s, half)
    rotate_into(b_refs, x_ref, moved(right, half), right)


def rotate(s, x, sizes):
    rows, cols = x.shape
    w = window(cols // 2)
    return pl.pallas_call(
        rotate_kernel,
        in_specs=whole(2),
        out_specs=whole(len(sizes)),
        out_shape=blocks_of(cols, sizes),
        cost_estimate=pl.CostEstimate(flops=2 * rows * cols * w, bytes_accessed=3 * rows * cols, transcendentals=0),
        compiler_params=params(),
        name="rotate",
    )(s, x)


def second_kernel(*refs):
    *parts, s_ref = refs
    rounded_factor(s_ref, cross_of(parts))


def second(parts):
    cols = parts[0].shape[1]
    w = window(cols // 2)
    return pl.pallas_call(
        second_kernel,
        in_specs=whole(len(parts)),
        out_specs=whole(1)[0],
        out_shape=jax.ShapeDtypeStruct((cols // 4, cols), BF16),
        cost_estimate=pl.CostEstimate(flops=8 * w**2, bytes_accessed=4 * w * w, transcendentals=0),
        compiler_params=params(),
        name="second",
    )(*parts)


def left_factor_kernel(s_ref, left_ref):
    left_ref[...] = left_columns(*factor(s_ref))


def columns_of(kernel, s):
    cols = s.shape[1]
    w = window(cols // 2)
    return pl.pallas_call(
        kernel,
        in_specs=whole(1),
        out_specs=whole(1)[0],
        out_shape=jax.ShapeDtypeStruct((cols, w), BF16),
        cost_estimate=pl.CostEstimate(flops=8 * w**3, bytes_accessed=4 * w * w, transcendentals=0),
        compiler_params=params(),
    )(s)


def pair_weight(q_ref, first):
    cols, w = q_ref.shape
    half = cols // 2
    rest = jnp.zeros((w - half, w), BF16)
    upper, lower = q_ref[:half], q_ref[half:]
    return jnp.concatenate([upper, rest, lower, rest] if first else [rest, upper, rest, lower], axis=0)


def pair_dot(a_refs, b_refs, start, stop, weight, first):
    w = weight.shape[1]
    cols = a_refs[0].shape[1]
    at = slice(0, w) if first else slice(cols - w, cols)
    a, b = span(a_refs, start, stop)[:, at], span(b_refs, start, stop)[:, at]
    return dot(jnp.concatenate([a, b], axis=1), weight, (1, 0))


def left_kernel(n_a, *refs):
    a_refs, (*b_refs, q_ref, o_ref) = refs[:n_a], refs[n_a:]
    rows = o_ref.shape[0] // 2
    for first in (True, False):
        weight = pair_weight(q_ref, first)
        for start, stop in spans(a_refs, b_refs):
            to = 0 if first else rows
            o_ref[to + start : to + stop, :] = low(pair_dot(a_refs, b_refs, start, stop, weight, first))


def left_half(a, b, q):
    rows, cols = sum(v.shape[0] for v in a), a[0].shape[1]
    w = q.shape[1]
    return pl.pallas_call(
        functools.partial(left_kernel, len(a)),
        in_specs=whole(len(a) + len(b) + 1),
        out_specs=whole(1)[0],
        out_shape=jax.ShapeDtypeStruct((2 * rows, w), BF16),
        cost_estimate=pl.CostEstimate(flops=8 * rows * w * w, bytes_accessed=6 * rows * cols, transcendentals=0),
        compiler_params=params(),
        name="left_half",
    )(*a, *b, q)


def final_kernel(base, cuts, n_a, *refs):
    a_refs, (b_ref, l_ref, q_ref, *_, o_ref, sem) = refs[:n_a], refs[n_a:]
    o_hbm = refs[n_a + 3] if base == 0 else refs[n_a + 4]
    if base == 0:
        refs[n_a + 4][...] = right_columns(*factor(q_ref))
        q_ref = refs[n_a + 4]
    rows, cols = l_ref.shape[0] // 2, o_ref.shape[1]
    copies = []
    for first in (True, False):
        weight = pair_weight(q_ref, first)
        for start, stop in cuts:
            a, b = span(a_refs, start, stop), b_ref.at[start - base : stop - base]
            right = pair_dot([a], [b], 0, stop - start, weight, first)
            to = slice(start, stop) if first else slice(rows + start, rows + stop)
            shift = -base if first else b_ref.shape[0] - base
            here = slice(start + shift, stop + shift)
            left = l_ref[to, :].astype(F32)
            packed_store(o_ref, here, left, right, cols // 2)
            copy = pltpu.make_async_copy(o_ref.at[here, :], o_hbm.at[to, :], sem.at[len(copies)])
            copy.start()
            copies.append(copy)
    for copy in copies:
        copy.wait()


def final(l, a, b, s):
    rows, cols, w = l.shape[0], a[0].shape[1], l.shape[1]
    result, weight, base = None, s, 0
    for block in b:
        n = block.shape[0]
        first = base == 0
        cuts = [(i, j) for i, j in spans(a, b) if base <= i < base + n]
        args = (*a, block, l, weight) + (() if first else (result,))
        result, *made = pl.pallas_call(
            functools.partial(final_kernel, base, cuts, len(a)),
            in_specs=whole(len(a) + 3) + ([] if first else [pl.BlockSpec(memory_space=pltpu.HBM)]),
            out_specs=[pl.BlockSpec(memory_space=pltpu.HBM)] + (whole(1) if first else []),
            out_shape=[jax.ShapeDtypeStruct((rows, cols), BF16)] + (blocks_of(w, [cols]) if first else []),
            input_output_aliases={} if first else {len(args) - 1: 0},
            scratch_shapes=[pltpu.VMEM((2 * n, cols), BF16), pltpu.SemaphoreType.DMA((2 * len(cuts),))],
            cost_estimate=pl.CostEstimate(flops=8 * n * w * w, bytes_accessed=8 * n * cols, transcendentals=0),
            compiler_params=params(),
            name="final",
        )(*args)
        weight = made[0] if first else weight
        base += n
    return result


def passed(x, by):
    n = lax.axis_size("pairs")
    return lax.ppermute(x, "pairs", [(i, (i + 2 * by) % n) for i in range(n)])


def row_parts(g):
    n = lax.axis_size("rows")
    if n & (n - 1) or n > 4:
        return [lax.psum(g.astype(F32), "rows")]
    return [g] + [lax.ppermute(g, "rows", [(i, i ^ k) for i in range(n)]) for k in range(1, n)]


def shares(rows, *parts):
    return [rows * e // 64 for e in parts]


def local(latent):
    rows = latent.shape[0] // 2
    head, middle, last = shares(rows, 34, 8, 22)
    raw_in = passed(taken(latent, last), 1)
    parts = row_parts(gram(latent, 4))
    s, share, a = rotor(parts, latent, [head, middle])
    share_in = passed(share, 1)
    a_in = [passed(a[0], 1)]
    a_in.append(passed(a[1], 1))
    b = rotate(s, latent, shares(rows, 42, 22))
    a.append(tail([s], latent, last))
    s_in = row_parts(share_in) if shared(latent.shape[1]) > 1 else [share_in]
    a_in.append(tail(s_in, raw_in, last))
    a_in[0], b_out = lax.optimization_barrier((a_in[0], b[0]))
    b_in = [passed(b_out, -1)]
    stats = gram_pair(a_in, b)
    parts = row_parts(stats)
    s = second(parts)
    s_in = passed(s, -1)
    s, *rest = lax.optimization_barrier((s, *b[1:]))
    for block in rest:
        b_in.append(passed(block, -1))
    left = columns_of(left_factor_kernel, s)
    return final(left_half(a_in, b, left), a, b_in, s_in)


def solution(mesh):
    return jax.shard_map(
        local,
        mesh=mesh,
        in_specs=(P("rows", "pairs"),),
        out_specs=P("rows", "pairs"),
        check_vma=False,
    )
```

profile of v0, /device:TPU:0, one launch (start us, length us, event | category | flops | bytes accessed | tf_op | source)
XLA Modules:
  0.0 80.2 jit_solution(5916203939312173310)
XLA Ops:
  0.0 0.0 copy-start
  0.0 1.4 %copy-done = bf16[2048,384]{1,0:T(8,128)(2,1)S(1)} copy-done((bf16[2048,384]{1,0:T(8,128)(2,1)S(1)}, bf16[2048,384]{1,0:T(8,128)(2,1)}, u32[]{:S(2)}) %copy-start) | copy-done | bytes 1572888
  1.4 0.5 gram.1.refs_0_
  1.9 0.0 copy-start.1
  2.0 4.0 %collective-permute-start.2 = (bf16[104,384]{1,0:T(8,128)(2,1)S(1)}, bf16[104,384]{1,0:T(8,128)(2,1)S(1)}, u32[]{:S(2)}, u32[]{:S(2)}) collective-permute-start(bf16[104,384]{1,0:T(8,128)(2,1)S(1)} %gram.1.refs_0_), channel_id=1, source_target_pairs={{0,24},{8,16},{16,8},{24,0},{1,25},{9,17},{17,9},{25,1},{2,26},{10... | collective-permute-start | bytes 239624 | tf_op jit(solution)/shard_map/ppermute | solution.py:520
  5.9 0.5 collective-permute-start.1
  6.5 0.1 collective-permute-start
  6.6 1.9 %collective-permute-done.2.refs_3_ = bf16[104,384]{1,0:T(8,128)(2,1)S(1)} collective-permute-done((bf16[104,384]{1,0:T(8,128)(2,1)S(1)}, bf16[104,384]{1,0:T(8,128)(2,1)S(1)}, u32[]{:S(2)}, u32[]{:S(2)}) %collective-permute-start.2) | collective-permute-done | bytes 79904 | tf_op jit(solution)/shard_map/ppermute | solution.py:520
  8.5 1.9 %collective-permute-done.1.refs_2_ = bf16[104,384]{1,0:T(8,128)(2,1)S(1)} collective-permute-done((bf16[104,384]{1,0:T(8,128)(2,1)S(1)}, bf16[104,384]{1,0:T(8,128)(2,1)S(1)}, u32[]{:S(2)}, u32[]{:S(2)}) %collective-permute-start.1) | collective-permute-done | bytes 79904 | tf_op jit(solution)/shard_map/ppermute | solution.py:520
  10.4 0.5 collective-permute-done.refs_1_
  10.9 1.9 %rotor.1 = (bf16[96,384]{1,0:T(8,128)(2,1)S(1)}, bf16[24,384]{1,0:T(8,128)(2,1)S(1)}, bf16[544,384]{1,0:T(8,128)(2,1)S(1)}, bf16[128,384]{1,0:T(8,128)(2,1)S(1)}) custom-call(bf16[104,384]{1,0:T(8,128)(2,1)S(1)} %gram.1.refs_0_, bf16[104,384]{1,0:T(8,128)(2,1)S(1)} %collective-permute-done.refs_1_, bf16[104,384]{1,0:T(8,128)(2,1)S(1)} %collective-permute-done.1.refs_2_, ...), custom_call_target="tpu_custom_call" | custom-call | flops 264241152 | bytes 1548288 | tf_op jit(solution)/shard_map/rotor/pallas_call | solution.py:335
  12.8 1.6 %collective-permute-start.3 = (bf16[544,384]{1,0:T(8,128)(2,1)S(1)}, bf16[544,384]{1,0:T(8,128)(2,1)S(1)}, u32[]{:S(2)}, u32[]{:S(2)}) collective-permute-start(bf16[544,384]{1,0:T(8,128)(2,1)S(1)} %get-tuple-element.17.refs_0_), channel_id=1, source_target_pairs={{0,2},{1,3},{2,4},{3,5},{4,6},{5,7},{6,0},{7,1},{8,10},{9,11},{10,... | collective-permute-start | bytes 1253384 | tf_op jit(solution)/shard_map/ppermute | solution.py:513
  14.4 1.1 %taken.1 = bf16[704,384]{1,0:T(8,128)(2,1)S(1)} custom-call(bf16[2048,384]{1,0:T(8,128)(2,1)} %x_hbm.1), custom_call_target="tpu_custom_call" | custom-call | bytes 1081344 | tf_op jit(solution)/shard_map/taken/pallas_call | solution.py:114
  15.5 1.6 %collective-permute-start.9 = (bf16[704,384]{1,0:T(8,128)(2,1)S(1)}, bf16[704,384]{1,0:T(8,128)(2,1)S(1)}, u32[]{:S(2)}, u32[]{:S(2)}) collective-permute-start(bf16[704,384]{1,0:T(8,128)(2,1)S(1)} %taken.1), channel_id=1, source_target_pairs={{0,2},{1,3},{2,4},{3,5},{4,6},{5,7},{6,0},{7,1},{8,10},{9,11},{10,... | collective-permute-start | bytes 1622024 | tf_op jit(solution)/shard_map/ppermute | solution.py:513
  17.1 0.0 copy-done.1
  17.1 1.8 %rotate.1 = (bf16[672,384]{1,0:T(8,128)(2,1)S(1)}, bf16[352,384]{1,0:T(8,128)(2,1)S(1)}) custom-call(bf16[96,384]{1,0:T(8,128)(2,1)S(1)} %get-tuple-element.19.refs_0_.s_ref, bf16[2048,384]{1,0:T(8,128)(2,1)S(1)} %copy-done.1), custom_call_target="tpu_custom_call" | custom-call | flops 402653184 | bytes 2359296 | tf_op jit(solution)/shard_map/rotate/pallas_call | solution.py:375
  18.9 8.4 %collective-permute-done.3.refs_0_ = bf16[544,384]{1,0:T(8,128)(2,1)S(1)} collective-permute-done((bf16[544,384]{1,0:T(8,128)(2,1)S(1)}, bf16[544,384]{1,0:T(8,128)(2,1)S(1)}, u32[]{:S(2)}, u32[]{:S(2)}) %collective-permute-start.3) | collective-permute-done | bytes 417824 | tf_op jit(solution)/shard_map/ppermute | solution.py:513
  27.4 1.6 %collective-permute-start.14 = (bf16[672,384]{1,0:T(8,128)(2,1)S(1)}, bf16[672,384]{1,0:T(8,128)(2,1)S(1)}, u32[]{:S(2)}, u32[]{:S(2)}) collective-permute-start(bf16[672,384]{1,0:T(8,128)(2,1)S(1)} %get-tuple-element.26.refs_3_), channel_id=1, source_target_pairs={{0,6},{1,7},{2,0},{3,1},{4,2},{5,3},{6,4},{7,5},{8,14},{9,15},{10,... | collective-permute-start | bytes 1548296 | tf_op jit(solution)/shard_map/ppermute | solution.py:513
  29.0 0.4 collective-permute-start.4
  29.4 0.0 collective-permute-start.5
  29.4 21.2 %collective-permute-done.5.refs_0_ = bf16[24,384]{1,0:T(8,128)(2,1)S(1)} collective-permute-done((bf16[24,384]{1,0:T(8,128)(2,1)S(1)}, bf16[24,384]{1,0:T(8,128)(2,1)S(1)}, u32[]{:S(2)}, u32[]{:S(2)}) %collective-permute-start.5) | collective-permute-done | bytes 18464 | tf_op jit(solution)/shard_map/ppermute | solution.py:513
  50.6 1.3 %collective-permute-start.8 = (bf16[24,384]{1,0:T(8,128)(2,1)S(1)}, bf16[24,384]{1,0:T(8,128)(2,1)S(1)}, u32[]{:S(2)}, u32[]{:S(2)}) collective-permute-start(bf16[24,384]{1,0:T(8,128)(2,1)S(1)} %collective-permute-done.5.refs_0_), channel_id=1, source_target_pairs={{0,24},{8,16},{16,8},{24,0},{1,25},{9,17},{17,9},{25,1},{2,26},{10... | collective-permute-start | bytes 55304 | tf_op jit(solution)/shard_map/ppermute | solution.py:520
  51.9 1.7 %collective-permute-start.7 = (bf16[24,384]{1,0:T(8,128)(2,1)S(1)}, bf16[24,384]{1,0:T(8,128)(2,1)S(1)}, u32[]{:S(2)}, u32[]{:S(2)}) collective-permute-start(bf16[24,384]{1,0:T(8,128)(2,1)S(1)} %collective-permute-done.5.refs_0_), channel_id=1, source_target_pairs={{0,16},{8,24},{16,0},{24,8},{1,17},{9,25},{17,1},{25,9},{2,18},{10... | collective-permute-start | bytes 55304 | tf_op jit(solution)/shard_map/ppermute | solution.py:520
  53.6 1.7 %collective-permute-done.8.refs_3_ = bf16[24,384]{1,0:T(8,128)(2,1)S(1)} collective-permute-done((bf16[24,384]{1,0:T(8,128)(2,1)S(1)}, bf16[24,384]{1,0:T(8,128)(2,1)S(1)}, u32[]{:S(2)}, u32[]{:S(2)}) %collective-permute-start.8) | collective-permute-done | bytes 18464 | tf_op jit(solution)/shard_map/ppermute | solution.py:520
  55.2 1.5 %collective-permute-start.6 = (bf16[24,384]{1,0:T(8,128)(2,1)S(1)}, bf16[24,384]{1,0:T(8,128)(2,1)S(1)}, u32[]{:S(2)}, u32[]{:S(2)}) collective-permute-start(bf16[24,384]{1,0:T(8,128)(2,1)S(1)} %collective-permute-done.5.refs_0_), channel_id=1, source_target_pairs={{0,8},{8,0},{16,24},{24,16},{1,9},{9,1},{17,25},{25,17},{2,10},{10... | collective-permute-start | bytes 55304 | tf_op jit(solution)/shard_map/ppermute | solution.py:520
  56.8 0.0 collective-permute-done.7.refs_2_
  56.8 2.2 %collective-permute-done.6.refs_1_ = bf16[24,384]{1,0:T(8,128)(2,1)S(1)} collective-permute-done((bf16[24,384]{1,0:T(8,128)(2,1)S(1)}, bf16[24,384]{1,0:T(8,128)(2,1)S(1)}, u32[]{:S(2)}, u32[]{:S(2)}) %collective-permute-start.6) | collective-permute-done | bytes 18464 | tf_op jit(solution)/shard_map/ppermute | solution.py:520
  59.0 0.0 collective-permute-done.9.refs_4_
  59.0 1.5 %tail.3.refs_2_ = bf16[352,384]{1,0:T(8,128)(2,1)S(1)} custom-call(bf16[24,384]{1,0:T(8,128)(2,1)S(1)} %collective-permute-done.5.refs_0_, bf16[24,384]{1,0:T(8,128)(2,1)S(1)} %collective-permute-done.6.refs_1_, bf16[24,384]{1,0:T(8,128)(2,1)S(1)} %collective-permute-done.7.refs_2_, bf16[24,384]{1,0:T(8,128)(2,1)S(1)} %collective-permute-done.8.refs_3_, ...), custom_call_target="tpu_custom_call" | custom-call | flops 138412032 | bytes 811008 | tf_op jit(solution)/shard_map/tail/pallas_call | solution.py:355
  60.5 0.0 collective-permute-done.4.refs_1_
  60.5 0.7 gram_pair.1.refs_0_
  61.2 1.4 %collective-permute-start.12 = (bf16[104,384]{1,0:T(8,128)(2,1)S(1)}, bf16[104,384]{1,0:T(8,128)(2,1)S(1)}, u32[]{:S(2)}, u32[]{:S(2)}) collective-permute-start(bf16[104,384]{1,0:T(8,128)(2,1)S(1)} %gram_pair.1.refs_0_), channel_id=1, source_target_pairs={{0,24},{8,16},{16,8},{24,0},{1,25},{9,17},{17,9},{25,1},{2,26},{10... | collective-permute-start | bytes 239624 | tf_op jit(solution)/shard_map/ppermute | solution.py:520
  62.6 1.7 %collective-permute-start.11 = (bf16[104,384]{1,0:T(8,128)(2,1)S(1)}, bf16[104,384]{1,0:T(8,128)(2,1)S(1)}, u32[]{:S(2)}, u32[]{:S(2)}) collective-permute-start(bf16[104,384]{1,0:T(8,128)(2,1)S(1)} %gram_pair.1.refs_0_), channel_id=1, source_target_pairs={{0,16},{8,24},{16,0},{24,8},{1,17},{9,25},{17,1},{25,9},{2,18},{10... | collective-permute-start | bytes 239624 | tf_op jit(solution)/shard_map/ppermute | solution.py:520
  64.3 0.5 collective-permute-start.10
  64.8 1.9 %collective-permute-done.12.refs_3_ = bf16[104,384]{1,0:T(8,128)(2,1)S(1)} collective-permute-done((bf16[104,384]{1,0:T(8,128)(2,1)S(1)}, bf16[104,384]{1,0:T(8,128)(2,1)S(1)}, u32[]{:S(2)}, u32[]{:S(2)}) %collective-permute-start.12) | collective-permute-done | bytes 79904 | tf_op jit(solution)/shard_map/ppermute | solution.py:520
  66.7 0.8 %collective-permute-done.11.refs_2_ = bf16[104,384]{1,0:T(8,128)(2,1)S(1)} collective-permute-done((bf16[104,384]{1,0:T(8,128)(2,1)S(1)}, bf16[104,384]{1,0:T(8,128)(2,1)S(1)}, u32[]{:S(2)}, u32[]{:S(2)}) %collective-permute-start.11) | collective-permute-done | bytes 79904 | tf_op jit(solution)/shard_map/ppermute | solution.py:520
  67.5 1.2 %collective-permute-done.10.refs_1_ = bf16[104,384]{1,0:T(8,128)(2,1)S(1)} collective-permute-done((bf16[104,384]{1,0:T(8,128)(2,1)S(1)}, bf16[104,384]{1,0:T(8,128)(2,1)S(1)}, u32[]{:S(2)}, u32[]{:S(2)}) %collective-permute-start.10) | collective-permute-done | bytes 79904 | tf_op jit(solution)/shard_map/ppermute | solution.py:520
  68.7 0.6 second.1.s_ref
  69.2 1.7 %collective-permute-start.13 = (bf16[352,384]{1,0:T(8,128)(2,1)S(1)}, bf16[352,384]{1,0:T(8,128)(2,1)S(1)}, u32[]{:S(2)}, u32[]{:S(2)}) collective-permute-start(bf16[352,384]{1,0:T(8,128)(2,1)S(1)} %get-tuple-element.24.refs_4_), channel_id=1, source_target_pairs={{0,6},{1,7},{2,0},{3,1},{4,2},{5,3},{6,4},{7,5},{8,14},{9,15},{10,... | collective-permute-start | bytes 811016 | tf_op jit(solution)/shard_map/ppermute | solution.py:513
  71.0 0.4 collective-permute-start.15
  71.4 1.4 %tail.2.refs_2_ = bf16[352,384]{1,0:T(8,128)(2,1)S(1)} custom-call(bf16[96,384]{1,0:T(8,128)(2,1)S(1)} %get-tuple-element.19.refs_0_.s_ref, bf16[2048,384]{1,0:T(8,128)(2,1)S(1)} %copy-done.1), custom_call_target="tpu_custom_call" | custom-call | flops 138412032 | bytes 811008 | tf_op jit(solution)/shard_map/tail/pallas_call | solution.py:355
  72.9 1.0 %shard_map.17.refs_5_ = bf16[384,256]{1,0:T(8,128)(2,1)S(1)} custom-call(bf16[96,384]{1,0:T(8,128)(2,1)S(1)} %second.1.s_ref), custom_call_target="tpu_custom_call" | custom-call | flops 134217728 | bytes 262144 | tf_op jit(solution)/shard_map/pallas_call | solution.py:412
  73.9 0.7 left_half.1.refs_4_
  74.6 1.9 %collective-permute-done.15.refs_5_ = bf16[96,384]{1,0:T(8,128)(2,1)S(1)} collective-permute-done((bf16[96,384]{1,0:T(8,128)(2,1)S(1)}, bf16[96,384]{1,0:T(8,128)(2,1)S(1)}, u32[]{:S(2)}, u32[]{:S(2)}) %collective-permute-start.15) | collective-permute-done | bytes 73760 | tf_op jit(solution)/shard_map/ppermute | solution.py:513
  76.6 0.0 collective-permute-done.14.refs_3_
  76.6 2.5 %final.2 = (bf16[2048,384]{1,0:T(8,128)(2,1)}, bf16[384,256]{1,0:T(8,128)(2,1)S(1)}) custom-call(bf16[544,384]{1,0:T(8,128)(2,1)S(1)} %get-tuple-element.17.refs_0_, bf16[128,384]{1,0:T(8,128)(2,1)S(1)} %get-tuple-element.18.refs_1_, bf16[352,384]{1,0:T(8,128)(2,1)S(1)} %tail.2.refs_2_, bf16[672,384]{1,0:T(8,128)(2,1)S(1)} %collective-permute-done.14.refs_3_, ...), custom_call_target="tpu_custom_call" | custom-call | flops 352321536 | bytes 2064384 | tf_op jit(solution)/shard_map/final/pallas_call | solution.py:495
  79.0 0.0 collective-permute-done.13.refs_3_
  79.0 1.2 %final.3 = bf16[2048,384]{1,0:T(8,128)(2,1)} custom-call(bf16[544,384]{1,0:T(8,128)(2,1)S(1)} %get-tuple-element.17.refs_0_, bf16[128,384]{1,0:T(8,128)(2,1)S(1)} %get-tuple-element.18.refs_1_, bf16[352,384]{1,0:T(8,128)(2,1)S(1)} %tail.2.refs_2_, bf16[352,384]{1,0:T(8,128)(2,1)S(1)} %collective-permute-done.13.refs_3_, ...), custom_call_target="tpu_custom_call", output_to_operand_aliasing={{}: (6, {})} | custom-call | flops 184549376 | bytes 1081344 | tf_op jit(solution)/shard_map/final/pallas_call | solution.py:495
Async XLA Ops:
  0.0 1.4 %copy-start = (bf16[2048,384]{1,0:T(8,128)(2,1)S(1)}, bf16[2048,384]{1,0:T(8,128)(2,1)}, u32[]{:S(2)}) copy-start(bf16[2048,384]{1,0:T(8,128)(2,1)} %x_hbm.1) | copy-start | bytes 4718596
  1.9 15.2 %copy-start.1 = (bf16[2048,384]{1,0:T(8,128)(2,1)S(1)}, bf16[2048,384]{1,0:T(8,128)(2,1)}, u32[]{:S(2)}) copy-start(bf16[2048,384]{1,0:T(8,128)(2,1)} %x_hbm.1) | copy-start | bytes 4718596
  2.0 6.5 %collective-permute-start.2 = (bf16[104,384]{1,0:T(8,128)(2,1)S(1)}, bf16[104,384]{1,0:T(8,128)(2,1)S(1)}, u32[]{:S(2)}, u32[]{:S(2)}) collective-permute-start(bf16[104,384]{1,0:T(8,128)(2,1)S(1)} %gram.1.refs_0_), channel_id=1, source_target_pairs={{0,24},{8,16},{16,8},{24,0},{1,25},{9,17},{17,9},{25,1},{2,26},{10... | collective-permute-start | bytes 239624 | tf_op jit(solution)/shard_map/ppermute | solution.py:520
  5.9 4.4 %collective-permute-start.1 = (bf16[104,384]{1,0:T(8,128)(2,1)S(1)}, bf16[104,384]{1,0:T(8,128)(2,1)S(1)}, u32[]{:S(2)}, u32[]{:S(2)}) collective-permute-start(bf16[104,384]{1,0:T(8,128)(2,1)S(1)} %gram.1.refs_0_), channel_id=1, source_target_pairs={{0,16},{8,24},{16,0},{24,8},{1,17},{9,25},{17,1},{25,9},{2,18},{10... | collective-permute-start | bytes 239624 | tf_op jit(solution)/shard_map/ppermute | solution.py:520
  6.5 4.4 %collective-permute-start = (bf16[104,384]{1,0:T(8,128)(2,1)S(1)}, bf16[104,384]{1,0:T(8,128)(2,1)S(1)}, u32[]{:S(2)}, u32[]{:S(2)}) collective-permute-start(bf16[104,384]{1,0:T(8,128)(2,1)S(1)} %gram.1.refs_0_), channel_id=1, source_target_pairs={{0,8},{8,0},{16,24},{24,16},{1,9},{9,1},{17,25},{25,17},{2,10},{10... | collective-permute-start | bytes 239624 | tf_op jit(solution)/shard_map/ppermute | solution.py:520
  12.8 14.5 %collective-permute-start.3 = (bf16[544,384]{1,0:T(8,128)(2,1)S(1)}, bf16[544,384]{1,0:T(8,128)(2,1)S(1)}, u32[]{:S(2)}, u32[]{:S(2)}) collective-permute-start(bf16[544,384]{1,0:T(8,128)(2,1)S(1)} %get-tuple-element.17.refs_0_), channel_id=1, source_target_pairs={{0,2},{1,3},{2,4},{3,5},{4,6},{5,7},{6,0},{7,1},{8,10},{9,11},{10,... | collective-permute-start | bytes 1253384 | tf_op jit(solution)/shard_map/ppermute | solution.py:513
  15.5 43.5 %collective-permute-start.9 = (bf16[704,384]{1,0:T(8,128)(2,1)S(1)}, bf16[704,384]{1,0:T(8,128)(2,1)S(1)}, u32[]{:S(2)}, u32[]{:S(2)}) collective-permute-start(bf16[704,384]{1,0:T(8,128)(2,1)S(1)} %taken.1), channel_id=1, source_target_pairs={{0,2},{1,3},{2,4},{3,5},{4,6},{5,7},{6,0},{7,1},{8,10},{9,11},{10,... | collective-permute-start | bytes 1622024 | tf_op jit(solution)/shard_map/ppermute | solution.py:513
  27.4 49.2 %collective-permute-start.14 = (bf16[672,384]{1,0:T(8,128)(2,1)S(1)}, bf16[672,384]{1,0:T(8,128)(2,1)S(1)}, u32[]{:S(2)}, u32[]{:S(2)}) collective-permute-start(bf16[672,384]{1,0:T(8,128)(2,1)S(1)} %get-tuple-element.26.refs_3_), channel_id=1, source_target_pairs={{0,6},{1,7},{2,0},{3,1},{4,2},{5,3},{6,4},{7,5},{8,14},{9,15},{10,... | collective-permute-start | bytes 1548296 | tf_op jit(solution)/shard_map/ppermute | solution.py:513
  29.0 31.5 %collective-permute-start.4 = (bf16[128,384]{1,0:T(8,128)(2,1)S(1)}, bf16[128,384]{1,0:T(8,128)(2,1)S(1)}, u32[]{:S(2)}, u32[]{:S(2)}) collective-permute-start(bf16[128,384]{1,0:T(8,128)(2,1)S(1)} %get-tuple-element.18.refs_1_), channel_id=1, source_target_pairs={{0,2},{1,3},{2,4},{3,5},{4,6},{5,7},{6,0},{7,1},{8,10},{9,11},{10,... | collective-permute-start | bytes 294920 | tf_op jit(solution)/shard_map/ppermute | solution.py:513
  29.4 21.2 %collective-permute-start.5 = (bf16[24,384]{1,0:T(8,128)(2,1)S(1)}, bf16[24,384]{1,0:T(8,128)(2,1)S(1)}, u32[]{:S(2)}, u32[]{:S(2)}) collective-permute-start(bf16[24,384]{1,0:T(8,128)(2,1)S(1)} %get-tuple-element.22), channel_id=1, source_target_pairs={{0,2},{1,3},{2,4},{3,5},{4,6},{5,7},{6,0},{7,1},{8,10},{9,11},{10,... | collective-permute-start | bytes 55304 | tf_op jit(solution)/shard_map/ppermute | solution.py:513
  50.6 4.7 %collective-permute-start.8 = (bf16[24,384]{1,0:T(8,128)(2,1)S(1)}, bf16[24,384]{1,0:T(8,128)(2,1)S(1)}, u32[]{:S(2)}, u32[]{:S(2)}) collective-permute-start(bf16[24,384]{1,0:T(8,128)(2,1)S(1)} %collective-permute-done.5.refs_0_), channel_id=1, source_target_pairs={{0,24},{8,16},{16,8},{24,0},{1,25},{9,17},{17,9},{25,1},{2,26},{10... | collective-permute-start | bytes 55304 | tf_op jit(solution)/shard_map/ppermute | solution.py:520
  51.9 4.9 %collective-permute-start.7 = (bf16[24,384]{1,0:T(8,128)(2,1)S(1)}, bf16[24,384]{1,0:T(8,128)(2,1)S(1)}, u32[]{:S(2)}, u32[]{:S(2)}) collective-permute-start(bf16[24,384]{1,0:T(8,128)(2,1)S(1)} %collective-permute-done.5.refs_0_), channel_id=1, source_target_pairs={{0,16},{8,24},{16,0},{24,8},{1,17},{9,25},{17,1},{25,9},{2,18},{10... | collective-permute-start | bytes 55304 | tf_op jit(solution)/shard_map/ppermute | solution.py:520
  55.2 3.8 %collective-permute-start.6 = (bf16[24,384]{1,0:T(8,128)(2,1)S(1)}, bf16[24,384]{1,0:T(8,128)(2,1)S(1)}, u32[]{:S(2)}, u32[]{:S(2)}) collective-permute-start(bf16[24,384]{1,0:T(8,128)(2,1)S(1)} %collective-permute-done.5.refs_0_), channel_id=1, source_target_pairs={{0,8},{8,0},{16,24},{24,16},{1,9},{9,1},{17,25},{25,17},{2,10},{10... | collective-permute-start | bytes 55304 | tf_op jit(solution)/shard_map/ppermute | solution.py:520
  61.2 5.4 %collective-permute-start.12 = (bf16[104,384]{1,0:T(8,128)(2,1)S(1)}, bf16[104,384]{1,0:T(8,128)(2,1)S(1)}, u32[]{:S(2)}, u32[]{:S(2)}) collective-permute-start(bf16[104,384]{1,0:T(8,128)(2,1)S(1)} %gram_pair.1.refs_0_), channel_id=1, source_target_pairs={{0,24},{8,16},{16,8},{24,0},{1,25},{9,17},{17,9},{25,1},{2,26},{10... | collective-permute-start | bytes 239624 | tf_op jit(solution)/shard_map/ppermute | solution.py:520
  62.6 4.8 %collective-permute-start.11 = (bf16[104,384]{1,0:T(8,128)(2,1)S(1)}, bf16[104,384]{1,0:T(8,128)(2,1)S(1)}, u32[]{:S(2)}, u32[]{:S(2)}) collective-permute-start(bf16[104,384]{1,0:T(8,128)(2,1)S(1)} %gram_pair.1.refs_0_), channel_id=1, source_target_pairs={{0,16},{8,24},{16,0},{24,8},{1,17},{9,25},{17,1},{25,9},{2,18},{10... | collective-permute-start | bytes 239624 | tf_op jit(solution)/shard_map/ppermute | solution.py:520
  64.3 4.4 %collective-permute-start.10 = (bf16[104,384]{1,0:T(8,128)(2,1)S(1)}, bf16[104,384]{1,0:T(8,128)(2,1)S(1)}, u32[]{:S(2)}, u32[]{:S(2)}) collective-permute-start(bf16[104,384]{1,0:T(8,128)(2,1)S(1)} %gram_pair.1.refs_0_), channel_id=1, source_target_pairs={{0,8},{8,0},{16,24},{24,16},{1,9},{9,1},{17,25},{25,17},{2,10},{10... | collective-permute-start | bytes 239624 | tf_op jit(solution)/shard_map/ppermute | solution.py:520
  69.2 9.8 %collective-permute-start.13 = (bf16[352,384]{1,0:T(8,128)(2,1)S(1)}, bf16[352,384]{1,0:T(8,128)(2,1)S(1)}, u32[]{:S(2)}, u32[]{:S(2)}) collective-permute-start(bf16[352,384]{1,0:T(8,128)(2,1)S(1)} %get-tuple-element.24.refs_4_), channel_id=1, source_target_pairs={{0,6},{1,7},{2,0},{3,1},{4,2},{5,3},{6,4},{7,5},{8,14},{9,15},{10,... | collective-permute-start | bytes 811016 | tf_op jit(solution)/shard_map/ppermute | solution.py:513
  71.0 5.6 %collective-permute-start.15 = (bf16[96,384]{1,0:T(8,128)(2,1)S(1)}, bf16[96,384]{1,0:T(8,128)(2,1)S(1)}, u32[]{:S(2)}, u32[]{:S(2)}) collective-permute-start(bf16[96,384]{1,0:T(8,128)(2,1)S(1)} %second.1.s_ref), channel_id=1, source_target_pairs={{0,6},{1,7},{2,0},{3,1},{4,2},{5,3},{6,4},{7,5},{8,14},{9,15},{10,... | collective-permute-start | bytes 221192 | tf_op jit(solution)/shard_map/ppermute | solution.py:513
where the time goes:
time: 80.4 us; the launch traced here: 80.2 us
  waiting for transfers between devices  43.7 us (54%)
  starting transfers between devices  20.1 us (25%)
  Pallas kernels  14.9 us (19%)
  local copies, waits for them, and re-layouts  1.41 us (2%)
    ppermute x7, waiting for transfers between devices, passed(): return lax.ppermute(x, 'pairs', [(i, (i + 2 * by) % n) for i in range(n)])  31.5 us
    ppermute x9, starting transfers between devices, row_parts(): lax.ppermute(g, 'rows', [(i, i ^ k) for i in range(n)])  12.7 us
    ppermute x9, waiting for transfers between devices, row_parts(): lax.ppermute(g, 'rows', [(i, i ^ k) for i in range(n)])  12.1 us
    ppermute x7, starting transfers between devices, passed(): return lax.ppermute(x, 'pairs', [(i, (i + 2 * by) % n) for i in range(n)])  7.46 us
    pallas_call x2, Pallas kernels, final(): pl.pallas_call(functools.partial(final_kernel, base, cuts, len(a)), in_sp...  3.63 us
    pallas_call x2, Pallas kernels, tail(): pl.pallas_call(tail_kernel, in_specs=whole(len(s) + 1), out_specs=whole(1...  2.91 us
    pallas_call x1, Pallas kernels, rotor(): pl.pallas_call(functools.partial(rotor_kernel, len(parts)), in_specs=whol...  1.93 us
    pallas_call x1, Pallas kernels, rotate(): pl.pallas_call(rotate_kernel, in_specs=whole(2), out_specs=whole(len(size...  1.79 us
  transfers between devices with their start and end apart: 16, of which 11 were waited for; matrix products, arithmetic and copies ran while one was open for 0% of the time, Pallas kernels for 14%

commit v1 on v0

--- a/solution.py
+++ b/solution.py
@@ -490,7 +490,11 @@
     for block in b:
         n = block.shape[0]
         first = base == 0
-        cuts = [(i, j) for i, j in spans(a, b) if base <= i < base + n]
+        cuts = []
+        for i, j in spans(a, b):
+            if base <= i < base + n:
+                middle = (i + j) // 2 if (j - i) % 32 == 0 else j
+                cuts += [(i, middle), (middle, j)] if middle < j else [(i, j)]
         args = (*a, block, l, weight) + (() if first else (result,))
         result, *made = pl.pallas_call(
             functools.partial(final_kernel, base, cuts, len(a)),

time: 80.4 us -> 80.2 us (level)
  no operation moved by 1% of the time
where the time goes in v1:
time: 80.2 us; the launch traced here: 80.1 us
  waiting for transfers between devices  43.7 us (54%)
  starting transfers between devices  20.1 us (25%)
  Pallas kernels  14.7 us (18%)
  local copies, waits for them, and re-layouts  1.41 us (2%)
    ppermute x7, waiting for transfers between devices, passed(): return lax.ppermute(x, 'pairs', [(i, (i + 2 * by) % n) for i in range(n)])  31.5 us
    ppermute x9, starting transfers between devices, row_parts(): lax.ppermute(g, 'rows', [(i, i ^ k) for i in range(n)])  12.7 us
    ppermute x9, waiting for transfers between devices, row_parts(): lax.ppermute(g, 'rows', [(i, i ^ k) for i in range(n)])  12.1 us
    ppermute x7, starting transfers between devices, passed(): return lax.ppermute(x, 'pairs', [(i, (i + 2 * by) % n) for i in range(n)])  7.46 us
    pallas_call x2, Pallas kernels, final(): pl.pallas_call(functools.partial(final_kernel, base, cuts, len(a)), in_sp...  3.48 us
    pallas_call x2, Pallas kernels, tail(): pl.pallas_call(tail_kernel, in_specs=whole(len(s) + 1), out_specs=whole(1...  2.91 us
    pallas_call x1, Pallas kernels, rotor(): pl.pallas_call(functools.partial(rotor_kernel, len(parts)), in_specs=whol...  1.93 us
    pallas_call x1, Pallas kernels, rotate(): pl.pallas_call(rotate_kernel, in_specs=whole(2), out_specs=whole(len(size...  1.79 us
  transfers between devices with their start and end apart: 16, of which 11 were waited for; matrix products, arithmetic and copies ran while one was open for 0% of the time, Pallas kernels for 14%

profile of v1, /device:TPU:0, one launch (start us, length us, event | category | flops | bytes accessed | tf_op | source)
XLA Modules:
  0.0 80.1 jit_solution(4844962122206606375)
XLA Ops:
  0.0 0.0 copy-start
  0.0 1.4 %copy-done = bf16[2048,384]{1,0:T(8,128)(2,1)S(1)} copy-done((bf16[2048,384]{1,0:T(8,128)(2,1)S(1)}, bf16[2048,384]{1,0:T(8,128)(2,1)}, u32[]{:S(2)}) %copy-start) | copy-done | bytes 1572888
  1.4 0.5 gram.1.refs_0_
  1.9 0.0 copy-start.1
  2.0 4.0 %collective-permute-start.2 = (bf16[104,384]{1,0:T(8,128)(2,1)S(1)}, bf16[104,384]{1,0:T(8,128)(2,1)S(1)}, u32[]{:S(2)}, u32[]{:S(2)}) collective-permute-start(bf16[104,384]{1,0:T(8,128)(2,1)S(1)} %gram.1.refs_0_), channel_id=1, source_target_pairs={{0,24},{8,16},{16,8},{24,0},{1,25},{9,17},{17,9},{25,1},{2,26},{10... | collective-permute-start | bytes 239624 | tf_op jit(solution)/shard_map/ppermute | solution.py:524
  5.9 0.5 collective-permute-start.1
  6.5 0.1 collective-permute-start
  6.6 1.9 %collective-permute-done.2.refs_3_ = bf16[104,384]{1,0:T(8,128)(2,1)S(1)} collective-permute-done((bf16[104,384]{1,0:T(8,128)(2,1)S(1)}, bf16[104,384]{1,0:T(8,128)(2,1)S(1)}, u32[]{:S(2)}, u32[]{:S(2)}) %collective-permute-start.2) | collective-permute-done | bytes 79904 | tf_op jit(solution)/shard_map/ppermute | solution.py:524
  8.5 1.9 %collective-permute-done.1.refs_2_ = bf16[104,384]{1,0:T(8,128)(2,1)S(1)} collective-permute-done((bf16[104,384]{1,0:T(8,128)(2,1)S(1)}, bf16[104,384]{1,0:T(8,128)(2,1)S(1)}, u32[]{:S(2)}, u32[]{:S(2)}) %collective-permute-start.1) | collective-permute-done | bytes 79904 | tf_op jit(solution)/shard_map/ppermute | solution.py:524
  10.4 0.5 collective-permute-done.refs_1_
  10.9 1.9 %rotor.1 = (bf16[96,384]{1,0:T(8,128)(2,1)S(1)}, bf16[24,384]{1,0:T(8,128)(2,1)S(1)}, bf16[544,384]{1,0:T(8,128)(2,1)S(1)}, bf16[128,384]{1,0:T(8,128)(2,1)S(1)}) custom-call(bf16[104,384]{1,0:T(8,128)(2,1)S(1)} %gram.1.refs_0_, bf16[104,384]{1,0:T(8,128)(2,1)S(1)} %collective-permute-done.refs_1_, bf16[104,384]{1,0:T(8,128)(2,1)S(1)} %collective-permute-done.1.refs_2_, ...), custom_call_target="tpu_custom_call" | custom-call | flops 264241152 | bytes 1548288 | tf_op jit(solution)/shard_map/rotor/pallas_call | solution.py:335
  12.8 1.6 %collective-permute-start.3 = (bf16[544,384]{1,0:T(8,128)(2,1)S(1)}, bf16[544,384]{1,0:T(8,128)(2,1)S(1)}, u32[]{:S(2)}, u32[]{:S(2)}) collective-permute-start(bf16[544,384]{1,0:T(8,128)(2,1)S(1)} %get-tuple-element.17.refs_0_), channel_id=1, source_target_pairs={{0,2},{1,3},{2,4},{3,5},{4,6},{5,7},{6,0},{7,1},{8,10},{9,11},{10,... | collective-permute-start | bytes 1253384 | tf_op jit(solution)/shard_map/ppermute | solution.py:517
  14.4 1.1 %taken.1 = bf16[704,384]{1,0:T(8,128)(2,1)S(1)} custom-call(bf16[2048,384]{1,0:T(8,128)(2,1)} %x_hbm.1), custom_call_target="tpu_custom_call" | custom-call | bytes 1081344 | tf_op jit(solution)/shard_map/taken/pallas_call | solution.py:114
  15.5 1.6 %collective-permute-start.9 = (bf16[704,384]{1,0:T(8,128)(2,1)S(1)}, bf16[704,384]{1,0:T(8,128)(2,1)S(1)}, u32[]{:S(2)}, u32[]{:S(2)}) collective-permute-start(bf16[704,384]{1,0:T(8,128)(2,1)S(1)} %taken.1), channel_id=1, source_target_pairs={{0,2},{1,3},{2,4},{3,5},{4,6},{5,7},{6,0},{7,1},{8,10},{9,11},{10,... | collective-permute-start | bytes 1622024 | tf_op jit(solution)/shard_map/ppermute | solution.py:517
  17.1 0.0 copy-done.1
  17.1 1.8 %rotate.1 = (bf16[672,384]{1,0:T(8,128)(2,1)S(1)}, bf16[352,384]{1,0:T(8,128)(2,1)S(1)}) custom-call(bf16[96,384]{1,0:T(8,128)(2,1)S(1)} %get-tuple-element.19.refs_0_.s_ref, bf16[2048,384]{1,0:T(8,128)(2,1)S(1)} %copy-done.1), custom_call_target="tpu_custom_call" | custom-call | flops 402653184 | bytes 2359296 | tf_op jit(solution)/shard_map/rotate/pallas_call | solution.py:375
  18.9 8.4 %collective-permute-done.3.refs_0_ = bf16[544,384]{1,0:T(8,128)(2,1)S(1)} collective-permute-done((bf16[544,384]{1,0:T(8,128)(2,1)S(1)}, bf16[544,384]{1,0:T(8,128)(2,1)S(1)}, u32[]{:S(2)}, u32[]{:S(2)}) %collective-permute-start.3) | collective-permute-done | bytes 417824 | tf_op jit(solution)/shard_map/ppermute | solution.py:517
  27.4 1.6 %collective-permute-start.14 = (bf16[672,384]{1,0:T(8,128)(2,1)S(1)}, bf16[672,384]{1,0:T(8,128)(2,1)S(1)}, u32[]{:S(2)}, u32[]{:S(2)}) collective-permute-start(bf16[672,384]{1,0:T(8,128)(2,1)S(1)} %get-tuple-element.26.refs_3_), channel_id=1, source_target_pairs={{0,6},{1,7},{2,0},{3,1},{4,2},{5,3},{6,4},{7,5},{8,14},{9,15},{10,... | collective-permute-start | bytes 1548296 | tf_op jit(solution)/shard_map/ppermute | solution.py:517
  29.0 0.4 collective-permute-start.4
  29.4 0.0 collective-permute-start.5
  29.4 21.2 %collective-permute-done.5.refs_0_ = bf16[24,384]{1,0:T(8,128)(2,1)S(1)} collective-permute-done((bf16[24,384]{1,0:T(8,128)(2,1)S(1)}, bf16[24,384]{1,0:T(8,128)(2,1)S(1)}, u32[]{:S(2)}, u32[]{:S(2)}) %collective-permute-start.5) | collective-permute-done | bytes 18464 | tf_op jit(solution)/shard_map/ppermute | solution.py:517
  50.6 1.3 %collective-permute-start.8 = (bf16[24,384]{1,0:T(8,128)(2,1)S(1)}, bf16[24,384]{1,0:T(8,128)(2,1)S(1)}, u32[]{:S(2)}, u32[]{:S(2)}) collective-permute-start(bf16[24,384]{1,0:T(8,128)(2,1)S(1)} %collective-permute-done.5.refs_0_), channel_id=1, source_target_pairs={{0,24},{8,16},{16,8},{24,0},{1,25},{9,17},{17,9},{25,1},{2,26},{10... | collective-permute-start | bytes 55304 | tf_op jit(solution)/shard_map/ppermute | solution.py:524
  51.9 1.7 %collective-permute-start.7 = (bf16[24,384]{1,0:T(8,128)(2,1)S(1)}, bf16[24,384]{1,0:T(8,128)(2,1)S(1)}, u32[]{:S(2)}, u32[]{:S(2)}) collective-permute-start(bf16[24,384]{1,0:T(8,128)(2,1)S(1)} %collective-permute-done.5.refs_0_), channel_id=1, source_target_pairs={{0,16},{8,24},{16,0},{24,8},{1,17},{9,25},{17,1},{25,9},{2,18},{10... | collective-permute-start | bytes 55304 | tf_op jit(solution)/shard_map/ppermute | solution.py:524
  53.6 1.7 %collective-permute-done.8.refs_3_ = bf16[24,384]{1,0:T(8,128)(2,1)S(1)} collective-permute-done((bf16[24,384]{1,0:T(8,128)(2,1)S(1)}, bf16[24,384]{1,0:T(8,128)(2,1)S(1)}, u32[]{:S(2)}, u32[]{:S(2)}) %collective-permute-start.8) | collective-permute-done | bytes 18464 | tf_op jit(solution)/shard_map/ppermute | solution.py:524
  55.2 1.5 %collective-permute-start.6 = (bf16[24,384]{1,0:T(8,128)(2,1)S(1)}, bf16[24,384]{1,0:T(8,128)(2,1)S(1)}, u32[]{:S(2)}, u32[]{:S(2)}) collective-permute-start(bf16[24,384]{1,0:T(8,128)(2,1)S(1)} %collective-permute-done.5.refs_0_), channel_id=1, source_target_pairs={{0,8},{8,0},{16,24},{24,16},{1,9},{9,1},{17,25},{25,17},{2,10},{10... | collective-permute-start | bytes 55304 | tf_op jit(solution)/shard_map/ppermute | solution.py:524
  56.8 0.0 collective-permute-done.7.refs_2_
  56.8 2.2 %collective-permute-done.6.refs_1_ = bf16[24,384]{1,0:T(8,128)(2,1)S(1)} collective-permute-done((bf16[24,384]{1,0:T(8,128)(2,1)S(1)}, bf16[24,384]{1,0:T(8,128)(2,1)S(1)}, u32[]{:S(2)}, u32[]{:S(2)}) %collective-permute-start.6) | collective-permute-done | bytes 18464 | tf_op jit(solution)/shard_map/ppermute | solution.py:524
  59.0 0.0 collective-permute-done.9.refs_4_
  59.0 1.5 %tail.3.refs_2_ = bf16[352,384]{1,0:T(8,128)(2,1)S(1)} custom-call(bf16[24,384]{1,0:T(8,128)(2,1)S(1)} %collective-permute-done.5.refs_0_, bf16[24,384]{1,0:T(8,128)(2,1)S(1)} %collective-permute-done.6.refs_1_, bf16[24,384]{1,0:T(8,128)(2,1)S(1)} %collective-permute-done.7.refs_2_, bf16[24,384]{1,0:T(8,128)(2,1)S(1)} %collective-permute-done.8.refs_3_, ...), custom_call_target="tpu_custom_call" | custom-call | flops 138412032 | bytes 811008 | tf_op jit(solution)/shard_map/tail/pallas_call | solution.py:355
  60.5 0.0 collective-permute-done.4.refs_1_
  60.5 0.7 gram_pair.1.refs_0_
  61.2 1.4 %collective-permute-start.12 = (bf16[104,384]{1,0:T(8,128)(2,1)S(1)}, bf16[104,384]{1,0:T(8,128)(2,1)S(1)}, u32[]{:S(2)}, u32[]{:S(2)}) collective-permute-start(bf16[104,384]{1,0:T(8,128)(2,1)S(1)} %gram_pair.1.refs_0_), channel_id=1, source_target_pairs={{0,24},{8,16},{16,8},{24,0},{1,25},{9,17},{17,9},{25,1},{2,26},{10... | collective-permute-start | bytes 239624 | tf_op jit(solution)/shard_map/ppermute | solution.py:524
  62.6 1.7 %collective-permute-start.11 = (bf16[104,384]{1,0:T(8,128)(2,1)S(1)}, bf16[104,384]{1,0:T(8,128)(2,1)S(1)}, u32[]{:S(2)}, u32[]{:S(2)}) collective-permute-start(bf16[104,384]{1,0:T(8,128)(2,1)S(1)} %gram_pair.1.refs_0_), channel_id=1, source_target_pairs={{0,16},{8,24},{16,0},{24,8},{1,17},{9,25},{17,1},{25,9},{2,18},{10... | collective-permute-start | bytes 239624 | tf_op jit(solution)/shard_map/ppermute | solution.py:524
  64.3 0.5 collective-permute-start.10
  64.8 1.9 %collective-permute-done.12.refs_3_ = bf16[104,384]{1,0:T(8,128)(2,1)S(1)} collective-permute-done((bf16[104,384]{1,0:T(8,128)(2,1)S(1)}, bf16[104,384]{1,0:T(8,128)(2,1)S(1)}, u32[]{:S(2)}, u32[]{:S(2)}) %collective-permute-start.12) | collective-permute-done | bytes 79904 | tf_op jit(solution)/shard_map/ppermute | solution.py:524
  66.7 0.8 %collective-permute-done.11.refs_2_ = bf16[104,384]{1,0:T(8,128)(2,1)S(1)} collective-permute-done((bf16[104,384]{1,0:T(8,128)(2,1)S(1)}, bf16[104,384]{1,0:T(8,128)(2,1)S(1)}, u32[]{:S(2)}, u32[]{:S(2)}) %collective-permute-start.11) | collective-permute-done | bytes 79904 | tf_op jit(solution)/shard_map/ppermute | solution.py:524
  67.5 1.2 %collective-permute-done.10.refs_1_ = bf16[104,384]{1,0:T(8,128)(2,1)S(1)} collective-permute-done((bf16[104,384]{1,0:T(8,128)(2,1)S(1)}, bf16[104,384]{1,0:T(8,128)(2,1)S(1)}, u32[]{:S(2)}, u32[]{:S(2)}) %collective-permute-start.10) | collective-permute-done | bytes 79904 | tf_op jit(solution)/shard_map/ppermute | solution.py:524
  68.7 0.6 second.1.s_ref
  69.2 1.7 %collective-permute-start.13 = (bf16[352,384]{1,0:T(8,128)(2,1)S(1)}, bf16[352,384]{1,0:T(8,128)(2,1)S(1)}, u32[]{:S(2)}, u32[]{:S(2)}) collective-permute-start(bf16[352,384]{1,0:T(8,128)(2,1)S(1)} %get-tuple-element.24.refs_4_), channel_id=1, source_target_pairs={{0,6},{1,7},{2,0},{3,1},{4,2},{5,3},{6,4},{7,5},{8,14},{9,15},{10,... | collective-permute-start | bytes 811016 | tf_op jit(solution)/shard_map/ppermute | solution.py:517
  71.0 0.4 collective-permute-start.15
  71.4 1.4 %tail.2.refs_2_ = bf16[352,384]{1,0:T(8,128)(2,1)S(1)} custom-call(bf16[96,384]{1,0:T(8,128)(2,1)S(1)} %get-tuple-element.19.refs_0_.s_ref, bf16[2048,384]{1,0:T(8,128)(2,1)S(1)} %copy-done.1), custom_call_target="tpu_custom_call" | custom-call | flops 138412032 | bytes 811008 | tf_op jit(solution)/shard_map/tail/pallas_call | solution.py:355
  72.9 1.0 %shard_map.17.refs_5_ = bf16[384,256]{1,0:T(8,128)(2,1)S(1)} custom-call(bf16[96,384]{1,0:T(8,128)(2,1)S(1)} %second.1.s_ref), custom_call_target="tpu_custom_call" | custom-call | flops 134217728 | bytes 262144 | tf_op jit(solution)/shard_map/pallas_call | solution.py:412
  73.9 0.7 left_half.1.refs_4_
  74.6 1.9 %collective-permute-done.15.refs_5_ = bf16[96,384]{1,0:T(8,128)(2,1)S(1)} collective-permute-done((bf16[96,384]{1,0:T(8,128)(2,1)S(1)}, bf16[96,384]{1,0:T(8,128)(2,1)S(1)}, u32[]{:S(2)}, u32[]{:S(2)}) %collective-permute-start.15) | collective-permute-done | bytes 73760 | tf_op jit(solution)/shard_map/ppermute | solution.py:517
  76.6 0.0 collective-permute-done.14.refs_3_
  76.6 2.4 %final.2 = (bf16[2048,384]{1,0:T(8,128)(2,1)}, bf16[384,256]{1,0:T(8,128)(2,1)S(1)}) custom-call(bf16[544,384]{1,0:T(8,128)(2,1)S(1)} %get-tuple-element.17.refs_0_, bf16[128,384]{1,0:T(8,128)(2,1)S(1)} %get-tuple-element.18.refs_1_, bf16[352,384]{1,0:T(8,128)(2,1)S(1)} %tail.2.refs_2_, bf16[672,384]{1,0:T(8,128)(2,1)S(1)} %collective-permute-done.14.refs_3_, ...), custom_call_target="tpu_custom_call" | custom-call | flops 352321536 | bytes 2064384 | tf_op jit(solution)/shard_map/final/pallas_call | solution.py:499
  79.0 0.0 collective-permute-done.13.refs_3_
  79.0 1.1 %final.3 = bf16[2048,384]{1,0:T(8,128)(2,1)} custom-call(bf16[544,384]{1,0:T(8,128)(2,1)S(1)} %get-tuple-element.17.refs_0_, bf16[128,384]{1,0:T(8,128)(2,1)S(1)} %get-tuple-element.18.refs_1_, bf16[352,384]{1,0:T(8,128)(2,1)S(1)} %tail.2.refs_2_, bf16[352,384]{1,0:T(8,128)(2,1)S(1)} %collective-permute-done.13.refs_3_, ...), custom_call_target="tpu_custom_call", output_to_operand_aliasing={{}: (6, {})} | custom-call | flops 184549376 | bytes 1081344 | tf_op jit(solution)/shard_map/final/pallas_call | solution.py:499
Async XLA Ops:
  0.0 1.4 %copy-start = (bf16[2048,384]{1,0:T(8,128)(2,1)S(1)}, bf16[2048,384]{1,0:T(8,128)(2,1)}, u32[]{:S(2)}) copy-start(bf16[2048,384]{1,0:T(8,128)(2,1)} %x_hbm.1) | copy-start | bytes 4718596
  1.9 15.2 %copy-start.1 = (bf16[2048,384]{1,0:T(8,128)(2,1)S(1)}, bf16[2048,384]{1,0:T(8,128)(2,1)}, u32[]{:S(2)}) copy-start(bf16[2048,384]{1,0:T(8,128)(2,1)} %x_hbm.1) | copy-start | bytes 4718596
  2.0 6.5 %collective-permute-start.2 = (bf16[104,384]{1,0:T(8,128)(2,1)S(1)}, bf16[104,384]{1,0:T(8,128)(2,1)S(1)}, u32[]{:S(2)}, u32[]{:S(2)}) collective-permute-start(bf16[104,384]{1,0:T(8,128)(2,1)S(1)} %gram.1.refs_0_), channel_id=1, source_target_pairs={{0,24},{8,16},{16,8},{24,0},{1,25},{9,17},{17,9},{25,1},{2,26},{10... | collective-permute-start | bytes 239624 | tf_op jit(solution)/shard_map/ppermute | solution.py:524
  5.9 4.4 %collective-permute-start.1 = (bf16[104,384]{1,0:T(8,128)(2,1)S(1)}, bf16[104,384]{1,0:T(8,128)(2,1)S(1)}, u32[]{:S(2)}, u32[]{:S(2)}) collective-permute-start(bf16[104,384]{1,0:T(8,128)(2,1)S(1)} %gram.1.refs_0_), channel_id=1, source_target_pairs={{0,16},{8,24},{16,0},{24,8},{1,17},{9,25},{17,1},{25,9},{2,18},{10... | collective-permute-start | bytes 239624 | tf_op jit(solution)/shard_map/ppermute | solution.py:524
  6.5 4.4 %collective-permute-start = (bf16[104,384]{1,0:T(8,128)(2,1)S(1)}, bf16[104,384]{1,0:T(8,128)(2,1)S(1)}, u32[]{:S(2)}, u32[]{:S(2)}) collective-permute-start(bf16[104,384]{1,0:T(8,128)(2,1)S(1)} %gram.1.refs_0_), channel_id=1, source_target_pairs={{0,8},{8,0},{16,24},{24,16},{1,9},{9,1},{17,25},{25,17},{2,10},{10... | collective-permute-start | bytes 239624 | tf_op jit(solution)/shard_map/ppermute | solution.py:524
  12.8 14.5 %collective-permute-start.3 = (bf16[544,384]{1,0:T(8,128)(2,1)S(1)}, bf16[544,384]{1,0:T(8,128)(2,1)S(1)}, u32[]{:S(2)}, u32[]{:S(2)}) collective-permute-start(bf16[544,384]{1,0:T(8,128)(2,1)S(1)} %get-tuple-element.17.refs_0_), channel_id=1, source_target_pairs={{0,2},{1,3},{2,4},{3,5},{4,6},{5,7},{6,0},{7,1},{8,10},{9,11},{10,... | collective-permute-start | bytes 1253384 | tf_op jit(solution)/shard_map/ppermute | solution.py:517
  15.5 43.5 %collective-permute-start.9 = (bf16[704,384]{1,0:T(8,128)(2,1)S(1)}, bf16[704,384]{1,0:T(8,128)(2,1)S(1)}, u32[]{:S(2)}, u32[]{:S(2)}) collective-permute-start(bf16[704,384]{1,0:T(8,128)(2,1)S(1)} %taken.1), channel_id=1, source_target_pairs={{0,2},{1,3},{2,4},{3,5},{4,6},{5,7},{6,0},{7,1},{8,10},{9,11},{10,... | collective-permute-start | bytes 1622024 | tf_op jit(solution)/shard_map/ppermute | solution.py:517
  27.4 49.2 %collective-permute-start.14 = (bf16[672,384]{1,0:T(8,128)(2,1)S(1)}, bf16[672,384]{1,0:T(8,128)(2,1)S(1)}, u32[]{:S(2)}, u32[]{:S(2)}) collective-permute-start(bf16[672,384]{1,0:T(8,128)(2,1)S(1)} %get-tuple-element.26.refs_3_), channel_id=1, source_target_pairs={{0,6},{1,7},{2,0},{3,1},{4,2},{5,3},{6,4},{7,5},{8,14},{9,15},{10,... | collective-permute-start | bytes 1548296 | tf_op jit(solution)/shard_map/ppermute | solution.py:517
  29.0 31.5 %collective-permute-start.4 = (bf16[128,384]{1,0:T(8,128)(2,1)S(1)}, bf16[128,384]{1,0:T(8,128)(2,1)S(1)}, u32[]{:S(2)}, u32[]{:S(2)}) collective-permute-start(bf16[128,384]{1,0:T(8,128)(2,1)S(1)} %get-tuple-element.18.refs_1_), channel_id=1, source_target_pairs={{0,2},{1,3},{2,4},{3,5},{4,6},{5,7},{6,0},{7,1},{8,10},{9,11},{10,... | collective-permute-start | bytes 294920 | tf_op jit(solution)/shard_map/ppermute | solution.py:517
  29.4 21.2 %collective-permute-start.5 = (bf16[24,384]{1,0:T(8,128)(2,1)S(1)}, bf16[24,384]{1,0:T(8,128)(2,1)S(1)}, u32[]{:S(2)}, u32[]{:S(2)}) collective-permute-start(bf16[24,384]{1,0:T(8,128)(2,1)S(1)} %get-tuple-element.22), channel_id=1, source_target_pairs={{0,2},{1,3},{2,4},{3,5},{4,6},{5,7},{6,0},{7,1},{8,10},{9,11},{10,... | collective-permute-start | bytes 55304 | tf_op jit(solution)/shard_map/ppermute | solution.py:517
  50.6 4.7 %collective-permute-start.8 = (bf16[24,384]{1,0:T(8,128)(2,1)S(1)}, bf16[24,384]{1,0:T(8,128)(2,1)S(1)}, u32[]{:S(2)}, u32[]{:S(2)}) collective-permute-start(bf16[24,384]{1,0:T(8,128)(2,1)S(1)} %collective-permute-done.5.refs_0_), channel_id=1, source_target_pairs={{0,24},{8,16},{16,8},{24,0},{1,25},{9,17},{17,9},{25,1},{2,26},{10... | collective-permute-start | bytes 55304 | tf_op jit(solution)/shard_map/ppermute | solution.py:524
  51.9 4.9 %collective-permute-start.7 = (bf16[24,384]{1,0:T(8,128)(2,1)S(1)}, bf16[24,384]{1,0:T(8,128)(2,1)S(1)}, u32[]{:S(2)}, u32[]{:S(2)}) collective-permute-start(bf16[24,384]{1,0:T(8,128)(2,1)S(1)} %collective-permute-done.5.refs_0_), channel_id=1, source_target_pairs={{0,16},{8,24},{16,0},{24,8},{1,17},{9,25},{17,1},{25,9},{2,18},{10... | collective-permute-start | bytes 55304 | tf_op jit(solution)/shard_map/ppermute | solution.py:524
  55.2 3.8 %collective-permute-start.6 = (bf16[24,384]{1,0:T(8,128)(2,1)S(1)}, bf16[24,384]{1,0:T(8,128)(2,1)S(1)}, u32[]{:S(2)}, u32[]{:S(2)}) collective-permute-start(bf16[24,384]{1,0:T(8,128)(2,1)S(1)} %collective-permute-done.5.refs_0_), channel_id=1, source_target_pairs={{0,8},{8,0},{16,24},{24,16},{1,9},{9,1},{17,25},{25,17},{2,10},{10... | collective-permute-start | bytes 55304 | tf_op jit(solution)/shard_map/ppermute | solution.py:524
  61.2 5.4 %collective-permute-start.12 = (bf16[104,384]{1,0:T(8,128)(2,1)S(1)}, bf16[104,384]{1,0:T(8,128)(2,1)S(1)}, u32[]{:S(2)}, u32[]{:S(2)}) collective-permute-start(bf16[104,384]{1,0:T(8,128)(2,1)S(1)} %gram_pair.1.refs_0_), channel_id=1, source_target_pairs={{0,24},{8,16},{16,8},{24,0},{1,25},{9,17},{17,9},{25,1},{2,26},{10... | collective-permute-start | bytes 239624 | tf_op jit(solution)/shard_map/ppermute | solution.py:524
  62.6 4.8 %collective-permute-start.11 = (bf16[104,384]{1,0:T(8,128)(2,1)S(1)}, bf16[104,384]{1,0:T(8,128)(2,1)S(1)}, u32[]{:S(2)}, u32[]{:S(2)}) collective-permute-start(bf16[104,384]{1,0:T(8,128)(2,1)S(1)} %gram_pair.1.refs_0_), channel_id=1, source_target_pairs={{0,16},{8,24},{16,0},{24,8},{1,17},{9,25},{17,1},{25,9},{2,18},{10... | collective-permute-start | bytes 239624 | tf_op jit(solution)/shard_map/ppermute | solution.py:524
  64.3 4.4 %collective-permute-start.10 = (bf16[104,384]{1,0:T(8,128)(2,1)S(1)}, bf16[104,384]{1,0:T(8,128)(2,1)S(1)}, u32[]{:S(2)}, u32[]{:S(2)}) collective-permute-start(bf16[104,384]{1,0:T(8,128)(2,1)S(1)} %gram_pair.1.refs_0_), channel_id=1, source_target_pairs={{0,8},{8,0},{16,24},{24,16},{1,9},{9,1},{17,25},{25,17},{2,10},{10... | collective-permute-start | bytes 239624 | tf_op jit(solution)/shard_map/ppermute | solution.py:524
  69.2 9.7 %collective-permute-start.13 = (bf16[352,384]{1,0:T(8,128)(2,1)S(1)}, bf16[352,384]{1,0:T(8,128)(2,1)S(1)}, u32[]{:S(2)}, u32[]{:S(2)}) collective-permute-start(bf16[352,384]{1,0:T(8,128)(2,1)S(1)} %get-tuple-element.24.refs_4_), channel_id=1, source_target_pairs={{0,6},{1,7},{2,0},{3,1},{4,2},{5,3},{6,4},{7,5},{8,14},{9,15},{10,... | collective-permute-start | bytes 811016 | tf_op jit(solution)/shard_map/ppermute | solution.py:517
  71.0 5.6 %collective-permute-start.15 = (bf16[96,384]{1,0:T(8,128)(2,1)S(1)}, bf16[96,384]{1,0:T(8,128)(2,1)S(1)}, u32[]{:S(2)}, u32[]{:S(2)}) collective-permute-start(bf16[96,384]{1,0:T(8,128)(2,1)S(1)} %second.1.s_ref), channel_id=1, source_target_pairs={{0,6},{1,7},{2,0},{3,1},{4,2},{5,3},{6,4},{7,5},{8,14},{9,15},{10,... | collective-permute-start | bytes 221192 | tf_op jit(solution)/shard_map/ppermute | solution.py:517
